TPU v7x, 128 devices: a whole 4x4x4 slice. The times are simulated.
128 devices in a mesh: group: 4 (over x_lo, core), tensor: 32 (over z, x_hi, y).
Axes of the slice: x: 4 (x_hi: 2, x_lo: 2; x = x_hi * 2 + x_lo), y: 4, z: 4, core: 2. Of those that a mesh axis runs over, the one named last changes fastest.
Arguments:
- hidden_in: bfloat16 [32768, 1536], P(('group', 'tensor')), may hold values from -6 to 6
- request_ids: int32 [128, 256], P(('group', 'tensor')), may hold values from 0 to 3, never falling along the last dimension, each value on 1 to 128 neighbouring positions
- norm_gains: float32 [2, 1536], replicated, may hold values from 0.5 to 1.5
- query_key_value_weight: bfloat16 [1536, 3072], replicated, may hold values from -0.15625 to 0.15625
- w_out: bfloat16 [1536, 1536], replicated, may hold values from -0.15625 to 0.15625
- w_in: bfloat16 [2, 1536, 4096], P(None, None, 'tensor'), may hold values from -0.15625 to 0.15625
- w_down: bfloat16 [4096, 1536], P('tensor'), may hold values from -0.09375 to 0.09375
- prefix_cache: bfloat16 [4, 1024, 1536], P('group', 'tensor'), may hold values from -210 to 210
- prefix_owner: int32 [32], replicated, may hold values from 0 to 3
- page_dest: int32 [2048, 1], P(('group', 'tensor')), may hold values from 0 to 3; in each aligned block of 16 rows (0 to 15, 16 to 31, ...) at most 8 rows name the same one
Outputs:
- hidden_out: bfloat16 [32768, 1536], P(('group', 'tensor'))
- suffix_cache: bfloat16 [4, 32, 4, 8, 16, 1536], P('group', 'tensor')
Inputs may be any that keep to these rules, and one draw needn't show every extreme that they name: `request_ids`: each row numbers its requests from 0 in order of tokens, never falling, each request holding 1 to 128 tokens. `prefix_owner`: each block of the prefix cache is read from the slot of its owner only. `page_dest`: among the 16 pages of one device at most 8 have the same destination, and exactly 8 in some devices.
All inputs are finite; a program needn't handle non-finite values.
Results may differ from a plain program's by a relative error of at most 0.013.
The roundings to bfloat16 on the way count: a program that leaves them out, or rounds other values in their place, can miss the bound.
Values may be sent and summed in bfloat16 or wider, within the bound.
A program may use at most 192 MiB of HBM per device.

v0:
```python
import jax
import jax.numpy as jnp
from jax import lax
from jax.sharding import PartitionSpec as P

QUERY_HEADS = 16
KEY_VALUE_HEADS = 8
HEAD_DIMENSION = 96
PREFIX_TOKENS = 1024
CAP = 8


ROPE_BASE = 100000.0
EPSILON = 1e-05
NEGATIVE_FILLER = -1e30


def from_root(shard, axis, root):
    mine = lax.axis_index(axis) == root
    return lax.psum(jnp.where(mine, shard, jnp.zeros_like(shard)), axis)


def rms_norm(inputs, gain_row):
    floated = inputs.astype(jnp.float32)
    return (
        floated
        * lax.rsqrt(jnp.mean(floated * floated, axis=-1, keepdims=True) + EPSILON)
        * gain_row
    )


def apply_rotary(head_values, locate_position):
    half_dim = head_values.shape[-1] // 2
    frequency = ROPE_BASE ** (-jnp.arange(half_dim, dtype=jnp.float32) / half_dim)
    angles = locate_position.astype(jnp.float32)[:, None] * frequency[None, :]
    cosine = jnp.cos(angles)[:, None, :]
    sine_part = jnp.sin(angles)[:, None, :]
    first_half = head_values[..., :half_dim]
    second_half = head_values[..., half_dim:]
    return jnp.concatenate(
        [
            first_half * cosine - second_half * sine_part,
            second_half * cosine + first_half * sine_part,
        ],
        axis=-1,
    )


def positions(segment):
    row_number = segment.shape[0]
    row_index = jnp.arange(row_number, dtype=jnp.int32)
    same_request = segment[:, None] == segment[None, :]
    first_row = jnp.min(jnp.where(same_request, row_index[None, :], row_number), axis=1)
    return PREFIX_TOKENS + row_index - first_row


def attend_update(attn_state, scores, value_head_rows):
    row_max, row_total, weighted = attn_state
    new_max = jnp.maximum(row_max, jnp.max(scores, axis=-1))
    weights = jnp.exp(scores - new_max[..., None])
    row_total = jnp.sum(weights, axis=-1)
    weighted = jnp.einsum(
        "rkgn,nkd->rkgd",
        weights.astype(jnp.bfloat16),
        value_head_rows,
        preferred_element_type=jnp.float32,
    )
    return (new_max, row_total, weighted)


def combine_states(left_state, right_state):
    new_max = jnp.maximum(left_state[0], right_state[0])
    left_factor = jnp.exp(left_state[0] - new_max)
    right_factor = jnp.exp(right_state[0] - new_max)
    row_total = left_state[1] * left_factor + right_state[1] * right_factor
    weighted = left_state[2] * left_factor[..., None] + right_state[2] * right_factor[..., None]
    return (new_max, row_total, weighted)


def expand_with(token_block, loaded_pages):
    gate_proj = jnp.dot(token_block, loaded_pages[0], preferred_element_type=jnp.float32)
    up_proj = jnp.dot(token_block, loaded_pages[1], preferred_element_type=jnp.float32)
    return (jax.nn.silu(gate_proj) * up_proj).astype(jnp.bfloat16)


def contract_with(activated, loaded_pages):
    return jnp.dot(activated, loaded_pages, preferred_element_type=jnp.float32)


def on_device(
    hidden_in,
    request_ids,
    norm_gains,
    query_key_value_weight,
    w_out,
    w_in,
    w_down,
    prefix_cache,
    prefix_owner,
    page_dest,
):
    token_rows = hidden_in.shape[0]
    query_columns = QUERY_HEADS * HEAD_DIMENSION
    key_value_width = KEY_VALUE_HEADS * HEAD_DIMENSION
    segment = request_ids[0]
    normed = rms_norm(hidden_in, norm_gains[0]).astype(jnp.bfloat16)
    projected_rows = jnp.dot(normed, query_key_value_weight, preferred_element_type=jnp.float32)
    locate_position = positions(segment)
    query_rows = apply_rotary(
        projected_rows[:, :query_columns].reshape(token_rows, QUERY_HEADS, HEAD_DIMENSION),
        locate_position,
    ).astype(jnp.bfloat16)
    fresh_keys = apply_rotary(
        projected_rows[:, query_columns : query_columns + key_value_width].reshape(
            token_rows, KEY_VALUE_HEADS, HEAD_DIMENSION
        ),
        locate_position,
    ).astype(jnp.bfloat16)
    fresh_values = (
        projected_rows[:, query_columns + key_value_width :]
        .reshape(token_rows, KEY_VALUE_HEADS, HEAD_DIMENSION)
        .astype(jnp.bfloat16)
    )
    query_groups = query_rows.reshape(
        token_rows, KEY_VALUE_HEADS, QUERY_HEADS // KEY_VALUE_HEADS, HEAD_DIMENSION
    )
    score_scale = HEAD_DIMENSION ** (-0.5)
    row_index = jnp.arange(token_rows, dtype=jnp.int32)
    allowed = (segment[None, :] == segment[:, None]) & (row_index[None, :] <= row_index[:, None])
    local_scores = (
        jnp.einsum("rkgd,nkd->rkgn", query_groups, fresh_keys, preferred_element_type=jnp.float32)
        * score_scale
    )
    local_scores = jnp.where(allowed[:, None, None, :], local_scores, NEGATIVE_FILLER)
    empty_state = (
        jnp.full(
            (token_rows, KEY_VALUE_HEADS, QUERY_HEADS // KEY_VALUE_HEADS),
            NEGATIVE_FILLER,
            jnp.float32,
        ),
        jnp.zeros((token_rows, KEY_VALUE_HEADS, QUERY_HEADS // KEY_VALUE_HEADS), jnp.float32),
        jnp.zeros(
            (token_rows, KEY_VALUE_HEADS, QUERY_HEADS // KEY_VALUE_HEADS, HEAD_DIMENSION),
            jnp.float32,
        ),
    )
    local_state = attend_update(empty_state, local_scores, fresh_values)
    owner_row = prefix_owner[lax.axis_index("tensor")]
    block_prefix = from_root(prefix_cache[0], "group", owner_row)
    loaded_pages = lax.all_gather(block_prefix, "tensor", axis=0, tiled=True)
    key_total = loaded_pages.shape[0]
    key_head_rows = loaded_pages[:, :key_value_width].reshape(
        key_total, KEY_VALUE_HEADS, HEAD_DIMENSION
    )
    value_head_rows = loaded_pages[:, key_value_width:].reshape(
        key_total, KEY_VALUE_HEADS, HEAD_DIMENSION
    )
    scores = (
        jnp.einsum(
            "rkgd,nkd->rkgn", query_groups, key_head_rows, preferred_element_type=jnp.float32
        )
        * score_scale
    )
    attn_state = attend_update(empty_state, scores, value_head_rows)
    attn_state = combine_states(attn_state, local_state)
    attended = (
        (attn_state[2] / attn_state[1][..., None])
        .reshape(token_rows, QUERY_HEADS * HEAD_DIMENSION)
        .astype(jnp.bfloat16)
    )
    middle = (
        hidden_in.astype(jnp.float32) + jnp.dot(attended, w_out, preferred_element_type=jnp.float32)
    ).astype(jnp.bfloat16)
    second = rms_norm(middle, norm_gains[1]).astype(jnp.bfloat16)
    activated = expand_with(second, lax.all_gather(w_in, "tensor", axis=2, tiled=True))
    mlp_out = contract_with(activated, lax.all_gather(w_down, "tensor", axis=0, tiled=True))
    hidden_out = (middle.astype(jnp.float32) + mlp_out).astype(jnp.bfloat16)
    cache_rows = jnp.concatenate(
        [
            fresh_keys.reshape(token_rows, key_value_width),
            fresh_values.reshape(token_rows, key_value_width),
        ],
        axis=1,
    )
    page_count = page_dest.shape[0]
    page_blocks = cache_rows.reshape(page_count, token_rows // page_count, 2 * key_value_width)
    destination = page_dest[:, 0]
    dest_count = lax.axis_size("group")
    group_iota = jnp.arange(dest_count, dtype=jnp.int32)
    onehot = (destination[:, None] == group_iota[None, :]).astype(jnp.int32)
    page_rank = jnp.sum((jnp.cumsum(onehot, axis=0) - onehot) * onehot, axis=1)
    slot_iota = jnp.arange(CAP, dtype=jnp.int32)
    select = (
        (destination[:, None, None] == group_iota[None, :, None])
        & (page_rank[:, None, None] == slot_iota[None, None, :])
    ).astype(jnp.bfloat16)
    outgoing = jnp.einsum(
        "pdj,pxc->djxc", select, page_blocks, preferred_element_type=jnp.float32
    ).astype(jnp.bfloat16)
    received = lax.all_to_all(outgoing, "group", split_axis=0, concat_axis=0, tiled=True)
    return (hidden_out, received[None, None])


def solution(mesh):
    return jax.shard_map(
        on_device,
        mesh=mesh,
        in_specs=(
            P(("group", "tensor"), None),
            P(("group", "tensor"), None),
            P(),
            P(),
            P(),
            P(None, None, "tensor"),
            P("tensor", None),
            P("group", "tensor", None),
            P(),
            P(("group", "tensor"), None),
        ),
        out_specs=(P(("group", "tensor"), None), P("group", "tensor", None, None, None, None)),
        check_vma=False,
    )
```

profile of v0, /device:TPU:1, one launch (start us, length us, event | category | flops | bytes accessed | tf_op | source)
XLA Modules:
  0.0 568.7 jit_solution(15678878967873433163)
XLA Ops:
  9.8 40.5 %all-reduce.2.cloned.1.call-done = bf16[32,1536]{1,0:T(8,128)(2,1)} async-done(((bf16[32,1536]{1,0:T(8,128)(2,1)}), bf16[32,1536]{1,0:T(8,128)(2,1)}) %all-reduce.2.cloned.1.call-update) | async-done | bytes 98320 | tf_op jit(solution)/shard_map/psum | solution.py:20
  51.6 1.4 slice_reduce_fusion
  54.4 5.5 fusion.36
  60.0 1.7 copy-done.1
  64.7 1.7 convolution_convert_fusion
  66.4 3.7 all-to-all-start
  70.1 2.7 slice.54
  73.7 1.9 copy.29
  77.5 1.9 fusion.16
  80.9 2.2 fusion.21
  83.2 8.6 %all-to-all-done = bf16[4,8,16,1536]{3,1,2,0:T(8,128)(2,1)S(1)} async-done(((bf16[4,8,16,1536]{3,1,2,0:T(8,128)(2,1)}), bf16[4,8,16,1536]{3,1,2,0:T(8,128)(2,1)S(1)}, u32[]{:S(2)}, u32[]{:S(2)}) %all-to-all-start) | async-done | bytes 1572896 | tf_op jit(solution)/shard_map/all_to_all | solution.py:200
  91.7 1.6 copy.38
  93.4 36.2 %all-gather.4.cloned.1.call-done = bf16[1024,1536]{1,0:T(8,128)(2,1)} async-done(((bf16[32,1536]{1,0:T(8,128)(2,1)}), bf16[1024,1536]{1,0:T(8,128)(2,1)}) %all-gather.4.cloned.1.call-update) | async-done | bytes 3145744 | tf_op jit(solution)/shard_map/all_gather | solution.py:150
  129.6 3.3 fusion.68
  132.9 1.8 copy.28
  134.6 1.6 copy.27
  136.3 9.7 %bitcast_reduce_fusion = (f32[256,8,2]{0,2,1:T(2,128)S(1)}, f32[8,1024,256,2]{2,1,3,0:T(8,128)}) fusion(bf16[1024,8,96,1]{0,2,3,1:T(8,128)(2,1)S(1)} %bitcast.100, bf16[256,8,2,48]{0,3,2,1:T(8,128)(2,1)} %bitcast.111, bf16[256,8,2,48]{0,3,2,1:T(8,128)(2,1)S(1)} %bitcast.109), kind=kOutput, calls=%fused_computation.1 | convolution fusion | flops 815263744 | bytes 19152896 | tf_op jit(solution)/shard_map/rkgd,nkd->rkgn/dot_general | solution.py:159
  146.0 8.7 %fusion.1 = f32[256,8,2]{0,2,1:T(2,128)S(1)} fusion(f32[8,1024,256,2]{2,1,3,0:T(8,128)} %get-tuple-element.24, f32[256,8,2]{0,2,1:T(2,128)S(1)} %broadcast_maximum_fusion.1), kind=kLoop, calls=%fused_computation.3 | loop fusion | flops 12578816 | bytes 16809984 | tf_op jit(solution)/shard_map/reduce_sum | solution.py:61
  154.9 9.1 %fusion.33 = bf16[256,8,2,96]{0,3,2,1:T(8,128)(2,1)S(1)} fusion(f32[8,96,256,2]{2,1,3,0:T(8,128)S(1)} %copy-done.4, bf16[1024,8,96,1]{0,2,3,1:T(8,128)(2,1)S(1)} %bitcast.106, f32[8,1024,256,2]{2,1,3,0:T(8,128)} %get-tuple-element.24, f32[256,8,2]{0,2,1:T(2,128)S(1)} %broadcast_maximum_fusion.1, f32[256,8,2]{0,2,1:T(2,128)S(1)} %get-tuple-element.8, ...), kind=kOutput, calls=%fused_computation.42 | convolution fusion | flops 819855360 | bytes 20774912 | tf_op jit(solution)/shard_map/rkgn,nkd->rkgd/dot_general | solution.py:62
  164.0 1.5 multiply_reduce_fusion
  165.5 252.4 %all-gather.6.cloned.1.call-done = bf16[2,1536,4096]{2,1,0:T(8,128)(2,1)} async-done(((bf16[2,1536,128]{2,1,0:T(8,128)(2,1)}), bf16[2,1536,4096]{2,1,0:T(8,128)(2,1)}) %all-gather.6.cloned.1.call-update) | async-done | bytes 25165840 | tf_op jit(solution)/shard_map/all_gather | solution.py:175
  417.9 10.2 %fusion.4 = f32[256,4096]{1,0:T(8,128)} fusion(bf16[2,1536,4096]{2,1,0:T(8,128)(2,1)} %all-gather.6.cloned.1.call-done, f32[256,1536]{1,0:T(8,128)S(1)} %get-tuple-element.26, f32[1536]{0:T(1024)S(1)} %copy-done.15, f32[256]{0:T(256)S(1)} %add_rsqrt_fusion), kind=kOutput, calls=%fused_computation.8 | convolution fusion | flops 3222405120 | bytes 18357248 | tf_op jit(solution)/shard_map/dot_general | solution.py:81
  428.2 120.1 %all-gather.8.cloned.1.call-done = bf16[4096,1536]{1,0:T(8,128)(2,1)} async-done(((bf16[128,1536]{1,0:T(8,128)(2,1)}), bf16[4096,1536]{1,0:T(8,128)(2,1)}) %all-gather.8.cloned.1.call-update) | async-done | bytes 12582928 | tf_op jit(solution)/shard_map/all_gather | solution.py:176
  548.3 13.9 %fusion.18 = bf16[256,1536]{1,0:T(8,128)(2,1)} fusion(f32[256,1536]{1,0:T(8,128)S(1)} %get-tuple-element.26, bf16[4096,1536]{1,0:T(8,128)(2,1)} %all-gather.8.cloned.1.call-done, bf16[2,1536,4096]{2,1,0:T(8,128)(2,1)} %all-gather.6.cloned.1.call-done, f32[256,4096]{1,0:T(8,128)} %fusion.4, f32[1536]{0:T(1024)S(1)} %copy-done.15, f32[256]{0:T(256)S(1)} %add_rsqrt_fusion), kind=kOutput, calls=%fused_computation.25 | convolution fusion | flops 6450708480 | bytes 33301504 | tf_op jit(solution)/shard_map/dot_general | solution.py:87
  (76 shorter events, 12.1 us)
Async XLA Ops:
  7.2 43.1 %all-reduce.2.cloned.1.call-start = ((), (), s32[]{:S(2)}) async-start(), calls=%async_computation.1 | async-start | bytes 196608 | tf_op jit(solution)/shard_map/psum | solution.py:20
  9.8 119.8 %all-gather.4.cloned.1.call-start = ((), (), s32[]{:S(2)}) async-start(), calls=%async_computation.2 | async-start | bytes 3244032 | tf_op jit(solution)/shard_map/all_gather | solution.py:150
  50.3 367.6 %all-gather.6.cloned.1.call-start = ((), (), s32[]{:S(2)}) async-start(), calls=%async_computation.3 | async-start | bytes 25952256 | tf_op jit(solution)/shard_map/all_gather | solution.py:175
  51.1 497.2 %all-gather.8.cloned.1.call-start = ((), (), s32[]{:S(2)}) async-start(), calls=%async_computation.4 | async-start | bytes 12976128 | tf_op jit(solution)/shard_map/all_gather | solution.py:176
  54.4 7.6 %copy-start.14 = (s32[1,256]{1,0:T(1,128)S(1)}, s32[1,256]{1,0:T(1,128)}, u32[]{:S(2)}) copy-start(s32[1,256]{1,0:T(1,128)} %param.11) | copy-start | bytes 3076
  59.9 1.7 copy-start.1
  61.7 2.7 copy-start.16
  62.4 0.6 copy-start.10
  62.4 0.6 copy-start.11
  62.5 0.7 copy-start.8
  62.6 0.8 copy-start.9
  66.4 25.3 %all-to-all-start = ((bf16[4,8,16,1536]{3,1,2,0:T(8,128)(2,1)}), bf16[4,8,16,1536]{3,1,2,0:T(8,128)(2,1)S(1)}, u32[]{:S(2)}, u32[]{:S(2)}) async-start(bf16[4,8,16,1536]{3,1,2,0:T(8,128)(2,1)} %convolution_convert_fusion), calls=%async_computation | async-start | bytes 3145728 | tf_op jit(solution)/shard_map/all_to_all | solution.py:200
  76.7 0.8 copy-start.5
  76.7 2.7 copy-start.7
  77.5 3.5 copy-start.3
  79.4 0.6 copy-start.12
  132.9 3.4 copy-start.6
  146.0 8.8 %copy-start.13 = (f32[256,8,2]{0,2,1:T(2,128)S(1)}, f32[256,8,2]{0,2,1:T(2,128)}, u32[]{:S(2)}) copy-start(f32[256,8,2]{0,2,1:T(2,128)} %copy-done.12) | copy-start | bytes 49156
  146.0 8.8 %copy-start.2 = (bf16[1024,768]{0,1:T(8,128)(2,1)S(1)}, bf16[1024,768]{0,1:T(8,128)(2,1)}, u32[]{:S(2)}) copy-start(bf16[1024,768]{0,1:T(8,128)(2,1)} %copy.27) | copy-start | bytes 4718596
  146.0 8.8 %copy-start.4 = (f32[8,96,256,2]{2,1,3,0:T(8,128)S(1)}, f32[8,96,256,2]{2,1,3,0:T(8,128)}, u32[]{:S(2)}) copy-start(f32[8,96,256,2]{2,1,3,0:T(8,128)} %fusion.21) | copy-start | bytes 4718596
  146.0 18.0 %slice-start = ((s8[4718592]{0:T(1024)(128)(4,1)}), s8[524288]{0:T(1024)(128)(4,1)S(1)}, s32[]{:S(2)}) async-start(s8[4718592]{0:T(1024)(128)(4,1)} %bitcast.98), calls=%async_computation.5 | async-start | bytes 1048576
  154.8 9.2 %slice-start.1 = ((s8[4718592]{0:T(1024)(128)(4,1)}), s8[4194304]{0:T(1024)(128)(4,1)S(1)}, s32[]{:S(2)}) async-start(s8[4718592]{0:T(1024)(128)(4,1)} %bitcast.98), calls=%async_computation.6 | async-start | bytes 8388608
  154.8 9.2 %copy-start = (bf16[256,1536]{1,0:T(8,128)(2,1)S(1)}, bf16[256,1536]{1,0:T(8,128)(2,1)}, u32[]{:S(2)}) copy-start(bf16[256,1536]{1,0:T(8,128)(2,1)} %param.10) | copy-start | bytes 2359300
  164.0 253.9 %copy-start.15 = (f32[1536]{0:T(1024)S(1)}, f32[1536]{0:T(1024)}, u32[]{:S(2)}) copy-start(f32[1536]{0:T(1024)} %get-tuple-element.6) | copy-start | bytes 18436
Sparse Core Ops, SparseCore 0:
  11.0 39.2 all-reduce.1
  53.3 76.2 all-gather.3
  132.3 285.5 all-gather.5
  420.8 127.4 all-gather.7
where the time goes:
time: 569 us
  waiting for transfers between devices  459 us (81%)
  matrix products  55.9 us (10%)
  local copies, waits for them, and re-layouts  21.6 us (4%)
  between operations  14.8 us (3%)
  other arithmetic  13.7 us (2%)
    all_gather x1, waiting for transfers between devices, on_device(): lax.all_gather(w_in, 'tensor', axis=2, tiled=True)  252 us
    all_gather x1, waiting for transfers between devices, on_device(): lax.all_gather(w_down, 'tensor', axis=0, tiled=True)  120 us
    psum x1, waiting for transfers between devices, from_root(): return lax.psum(jnp.where(mine, shard, jnp.zeros_like(shard)), axis)  40.5 us
    all_gather x1, waiting for transfers between devices, on_device(): loaded_pages = lax.all_gather(block_prefix, 'tensor', axis=0, tiled=True)  36.2 us
    dot_general x1, matrix products, contract_with(): return jnp.dot(activated, loaded_pages, preferred_element_type=jnp.float32)  13.9 us
  transfers between devices with their start and end apart: 5, of which 5 were waited for; matrix products, arithmetic and copies ran while one was open for 13% of the time, Pallas kernels for 0%

commit v1 on v0

--- a/solution.py
+++ b/solution.py
@@ -1,6 +1,10 @@
+import functools
+
 import jax
 import jax.numpy as jnp
 from jax import lax
+from jax.experimental import pallas as pl
+from jax.experimental.pallas import tpu as pltpu
 from jax.sharding import PartitionSpec as P
 
 QUERY_HEADS = 16
@@ -8,6 +12,9 @@
 HEAD_DIMENSION = 96
 PREFIX_TOKENS = 1024
 CAP = 8
+WIDTH = 1536
+HALF = 768
+MESH = pl.DeviceIdType.MESH
 
 
 ROPE_BASE = 100000.0
@@ -15,9 +22,208 @@
 NEGATIVE_FILLER = -1e30
 
 
-def from_root(shard, axis, root):
-    mine = lax.axis_index(axis) == root
-    return lax.psum(jnp.where(mine, shard, jnp.zeros_like(shard)), axis)
+N_Z, N_H, N_Y = 4, 2, 4
+DIRECTIONS = ("x", "y+", "y-", "z+", "z-", "sib")
+ALL = slice(None)
+
+
+class Plan:
+    def __init__(self):
+        self.copies = []
+
+    def add(self, buffer, source, target, direction, after, size):
+        self.copies.append((buffer, source, target, direction, tuple(after), size))
+        return len(self.copies) - 1
+
+    def ring(self, buffer, axis, after, block, size):
+        up = self.add(buffer, block(0, None), block(3, None), axis + "+", after, size)
+        down = self.add(buffer, block(0, None), block(1, None), axis + "-", after, size)
+        far_up = self.add(buffer, block(3, 0), block(2, 0), axis + "+", [up], size / 2)
+        far_down = self.add(buffer, block(1, 1), block(2, 1), axis + "-", [down], size / 2)
+        return [up, down, far_up, far_down]
+
+    def piece(self, buffer, order, cut, size, after=()):
+        index = lambda z, h, y, part: (z, h, y) + cut(part)
+        done = []
+        if order[0] == "x":
+            swap = self.add(buffer, index(0, 0, 0, None), index(0, 1, 0, None), "x", after, size)
+            done.append(swap)
+            for h, first in ((0, list(after)), (1, [swap])):
+                if order[1] == "y":
+                    near = self.ring(buffer, "y", first, lambda d, p, h=h: index(0, h, d, p), size)
+                    far = self.ring(buffer, "z", near, lambda d, p, h=h: index(d, h, ALL, p), 4 * size)
+                else:
+                    near = self.ring(buffer, "z", first, lambda d, p, h=h: index(d, h, 0, p), size)
+                    far = self.ring(buffer, "y", near, lambda d, p, h=h: index(ALL, h, d, p), 4 * size)
+                done += near + far
+        else:
+            if order[0] == "y":
+                near = self.ring(buffer, "y", list(after), lambda d, p: index(0, 0, d, p), size)
+                far = self.ring(buffer, "z", near, lambda d, p: index(d, 0, ALL, p), 4 * size)
+                at = lambda d, h: index(d, h, ALL, None)
+            else:
+                near = self.ring(buffer, "z", list(after), lambda d, p: index(d, 0, 0, p), size)
+                far = self.ring(buffer, "y", near, lambda d, p: index(ALL, 0, d, p), 4 * size)
+                at = lambda d, h: index(ALL, h, d, None)
+            done += near + far
+            for d, need in ((0, near), (3, far[:1]), (1, far[1:2]), (2, far[2:])):
+                done.append(self.add(buffer, at(d, 0), at(d, 1), "x", need, 4 * size))
+        return done
+
+    def order(self, link=46.0, chip=250.0, latency=1600.0):
+        free = {d: 0.0 for d in DIRECTIONS}
+        arrival, issued, left, now = {}, [], list(range(len(self.copies))), 0.0
+        while left:
+            ready = {k: max([now] + [arrival[d] for d in self.copies[k][4]]) for k in left
+                     if all(d in arrival for d in self.copies[k][4])}
+            pick = min(ready, key=lambda k: (ready[k], k))
+            now = ready[pick]
+            direction, size = self.copies[pick][3], self.copies[pick][5]
+            start = max(now, free[direction])
+            free[direction] = start + size / (chip if direction == "sib" else link)
+            arrival[pick] = free[direction] + latency
+            issued.append(pick)
+            left.remove(pick)
+        return issued, arrival
+
+
+def gather_plan():
+    plan = Plan()
+
+    def prefix_cut(first):
+        return lambda part: (
+            pl.ds(first, 16),
+            pl.ds(0, HALF) if part is None else pl.ds(384 * part, 384),
+        )
+
+    def row_cut(first, count):
+        return lambda part: (
+            pl.ds(first, count) if part is None else pl.ds(first + count // 2 * part, count // 2),
+            ALL,
+        )
+
+    done = plan.piece("prefix", "xyz", prefix_cut(0), 16 * HALF * 2)
+    done += plan.piece("prefix", "xzy", prefix_cut(16), 16 * HALF * 2)
+    plan.add("prefix", (), (), "sib", done, 32 * 32 * HALF * 2)
+    plan.piece("in", "xyz", row_cut(0, HALF), HALF * 256)
+    plan.piece("in", "xzy", row_cut(HALF, HALF), HALF * 256)
+    plan.piece("down", "yzx", row_cut(0, 32), 32 * WIDTH * 2)
+    plan.piece("down", "zyx", row_cut(32, 32), 32 * WIDTH * 2)
+    return plan
+
+
+def neighbours():
+    g, t = lax.axis_index("group"), lax.axis_index("tensor")
+    core, low = g % 2, g // 2
+    y, high, z = t % 4, (t // 4) % 2, t // 8
+
+    def at(zz, hh, yy):
+        return (zz % 4) * 8 + hh * 4 + yy % 4
+
+    return {
+        "x": ((1 - low) * 2 + core, at(z, 1 - high, y)),
+        "y+": (g, at(z, high, y + 1)),
+        "y-": (g, at(z, high, y + 3)),
+        "z+": (g, at(z + 1, high, y)),
+        "z-": (g, at(z + 3, high, y)),
+        "sib": (low * 2 + 1 - core, t),
+        "twin": ((1 - low) * 2 + core, t),
+        "cross": ((1 - low) * 2 + 1 - core, t),
+    }
+
+
+def gather_kernel(
+    owned, block, win, wdown, pages_ref, win_ref, wdown_ref, rival, chosen, local, cand_send, cand_recv, send, recv
+):
+    core = lax.axis_index("group") % 2
+    near = neighbours()
+    barrier = pltpu.get_barrier_semaphore()
+    for target in near.values():
+        pl.semaphore_signal(barrier, inc=1, device_id=target, device_id_type=MESH)
+    pl.semaphore_wait(barrier, len(near))
+
+    plan = gather_plan()
+    own = [
+        pltpu.make_async_copy(win, win_ref.at[0, 0, 0], local.at[0]),
+        pltpu.make_async_copy(wdown, wdown_ref.at[0, 0, 0], local.at[1]),
+    ]
+    rivals = [
+        pltpu.make_async_remote_copy(
+            src_ref=block.at[half],
+            dst_ref=rival.at[slot],
+            send_sem=cand_send.at[slot],
+            recv_sem=cand_recv.at[slot],
+            device_id=near[name],
+            device_id_type=MESH,
+        )
+        for slot, (name, half) in enumerate((("sib", 1 - core), ("twin", core), ("cross", 1 - core)))
+    ]
+    for copy in rivals + own:
+        copy.start()
+    total = jnp.where(owned[0] > 0.5, block[core], jnp.zeros_like(block[core]))
+    for slot, copy in enumerate(rivals):
+        copy.wait_recv()
+        total = jnp.where(owned[slot + 1] > 0.5, rival[slot], total)
+    chosen[...] = total
+    last = pltpu.make_async_copy(chosen, pages_ref.at[core, 0, 0, 0], local.at[2])
+    last.start()
+    for copy in own + [last]:
+        copy.wait()
+
+    def place(name, index):
+        if name == "prefix":
+            return pages_ref.at[core].at[index] if index else pages_ref.at[core]
+        return {"in": win_ref, "down": wdown_ref}[name].at[index]
+
+    order, _ = plan.order()
+    copies, arrived = {}, set()
+    for k in order:
+        name, source, target, direction, after, _ = plan.copies[k]
+        for other in after:
+            if other not in arrived:
+                copies[other].wait_recv()
+                arrived.add(other)
+        copies[k] = pltpu.make_async_remote_copy(
+            src_ref=place(name, source),
+            dst_ref=place(name, target),
+            send_sem=send.at[k],
+            recv_sem=recv.at[k],
+            device_id=near[direction],
+            device_id_type=MESH,
+        )
+        copies[k].start()
+    for k in order:
+        if k not in arrived:
+            copies[k].wait_recv()
+    for k in order:
+        copies[k].wait_send()
+    for copy in rivals:
+        copy.wait_send()
+
+
+def gather(owned, block, win, wdown):
+    count = len(gather_plan().copies)
+    vmem = pl.BlockSpec(memory_space=pltpu.VMEM)
+    return pl.pallas_call(
+        gather_kernel,
+        out_shape=(
+            jax.ShapeDtypeStruct((2, 4, 2, 4, 32, HALF), jnp.bfloat16),
+            jax.ShapeDtypeStruct((4, 2, 4, WIDTH, 128), jnp.bfloat16),
+            jax.ShapeDtypeStruct((4, 2, 4, 64, WIDTH), jnp.bfloat16),
+        ),
+        in_specs=[vmem] * 4,
+        out_specs=(pl.BlockSpec(memory_space=pl.ANY),) * 3,
+        scratch_shapes=[
+            pltpu.VMEM((3, 32, HALF), jnp.bfloat16),
+            pltpu.VMEM((32, HALF), jnp.bfloat16),
+            pltpu.SemaphoreType.DMA((3,)),
+            pltpu.SemaphoreType.DMA((3,)),
+            pltpu.SemaphoreType.DMA((3,)),
+            pltpu.SemaphoreType.DMA((count,)),
+            pltpu.SemaphoreType.DMA((count,)),
+        ],
+        compiler_params=pltpu.CompilerParams(collective_id=0, has_side_effects=True),
+    )(owned, block, win, wdown)
 
 
 def rms_norm(inputs, gain_row):
@@ -77,14 +283,9 @@
     return (new_max, row_total, weighted)
 
 
-def expand_with(token_block, loaded_pages):
-    gate_proj = jnp.dot(token_block, loaded_pages[0], preferred_element_type=jnp.float32)
-    up_proj = jnp.dot(token_block, loaded_pages[1], preferred_element_type=jnp.float32)
-    return (jax.nn.silu(gate_proj) * up_proj).astype(jnp.bfloat16)
-
-
-def contract_with(activated, loaded_pages):
-    return jnp.dot(activated, loaded_pages, preferred_element_type=jnp.float32)
+def sibling_swap(array):
+    pairs = [(0, 1), (1, 0), (2, 3), (3, 2)]
+    return lax.ppermute(array, "group", pairs)
 
 
 def on_device(
@@ -102,6 +303,18 @@
     token_rows = hidden_in.shape[0]
     query_columns = QUERY_HEADS * HEAD_DIMENSION
     key_value_width = KEY_VALUE_HEADS * HEAD_DIMENSION
+    me = lax.axis_index("group")
+    core = me % 2
+    owner_row = prefix_owner[lax.axis_index("tensor")]
+    owned = jnp.broadcast_to(
+        (owner_row == jnp.bitwise_xor(me, jnp.arange(4, dtype=jnp.int32)))[:, None, None], (4, 1, HALF)
+    ).astype(jnp.float32)
+    win = lax.dynamic_slice_in_dim(w_in, 64 * core, 64, axis=2)
+    win = jnp.concatenate([win[0], win[1]], axis=1)
+    wdown = lax.dynamic_slice_in_dim(w_down, 64 * core, 64, axis=0)
+    block = jnp.stack([prefix_cache[0][:, :HALF], prefix_cache[0][:, HALF:]])
+    pages, win, wdown = gather(owned, block, win, wdown)
+
     segment = request_ids[0]
     normed = rms_norm(hidden_in, norm_gains[0]).astype(jnp.bfloat16)
     projected_rows = jnp.dot(normed, query_key_value_weight, preferred_element_type=jnp.float32)
@@ -138,23 +351,12 @@
             NEGATIVE_FILLER,
             jnp.float32,
         ),
-        jnp.zeros((token_rows, KEY_VALUE_HEADS, QUERY_HEADS // KEY_VALUE_HEADS), jnp.float32),
-        jnp.zeros(
-            (token_rows, KEY_VALUE_HEADS, QUERY_HEADS // KEY_VALUE_HEADS, HEAD_DIMENSION),
-            jnp.float32,
-        ),
+        None,
+        None,
     )
     local_state = attend_update(empty_state, local_scores, fresh_values)
-    owner_row = prefix_owner[lax.axis_index("tensor")]
-    block_prefix = from_root(prefix_cache[0], "group", owner_row)
-    loaded_pages = lax.all_gather(block_prefix, "tensor", axis=0, tiled=True)
-    key_total = loaded_pages.shape[0]
-    key_head_rows = loaded_pages[:, :key_value_width].reshape(
-        key_total, KEY_VALUE_HEADS, HEAD_DIMENSION
-    )
-    value_head_rows = loaded_pages[:, key_value_width:].reshape(
-        key_total, KEY_VALUE_HEADS, HEAD_DIMENSION
-    )
+    key_head_rows = pages[0].reshape(PREFIX_TOKENS, KEY_VALUE_HEADS, HEAD_DIMENSION)
+    value_head_rows = pages[1].reshape(PREFIX_TOKENS, KEY_VALUE_HEADS, HEAD_DIMENSION)
     scores = (
         jnp.einsum(
             "rkgd,nkd->rkgn", query_groups, key_head_rows, preferred_element_type=jnp.float32
@@ -172,8 +374,14 @@
         hidden_in.astype(jnp.float32) + jnp.dot(attended, w_out, preferred_element_type=jnp.float32)
     ).astype(jnp.bfloat16)
     second = rms_norm(middle, norm_gains[1]).astype(jnp.bfloat16)
-    activated = expand_with(second, lax.all_gather(w_in, "tensor", axis=2, tiled=True))
-    mlp_out = contract_with(activated, lax.all_gather(w_down, "tensor", axis=0, tiled=True))
+    both = jnp.concatenate([second, sibling_swap(second)], axis=0)
+    win = win.reshape(32, WIDTH, 128)
+    product = jnp.einsum("mk,skn->smn", both, win, preferred_element_type=jnp.float32)
+    activated = (jax.nn.silu(product[..., :64]) * product[..., 64:]).astype(jnp.bfloat16)
+    partial = jnp.einsum(
+        "smn,snd->md", activated, wdown.reshape(32, 64, WIDTH), preferred_element_type=jnp.float32
+    )
+    mlp_out = partial[:token_rows] + sibling_swap(partial[token_rows:])
     hidden_out = (middle.astype(jnp.float32) + mlp_out).astype(jnp.bfloat16)
     cache_rows = jnp.concatenate(
         [

time: 569 us -> 221 us (0.39)
  waiting for transfers between devices: 459 us -> 0.84 us
  Pallas kernels: 0 us -> 112 us
  blocking collectives: 0 us -> 21.6 us
  between operations: 14.8 us -> 1.09 us
  matrix products: 55.9 us -> 42.2 us
  other arithmetic: 13.7 us -> 19.5 us
    all_gather x3 -> x0, waiting for transfers between devices: 409 us -> none  [the longest x1 252 us: on_device(): lax.all_gather(w_in, 'tensor', axis=2, tiled=True)]
    pallas_call x0 -> x1, Pallas kernels: none -> 112 us  [gather(): pl.pallas_call(gather_kernel, out_shape=(jax.ShapeDtypeStruct((2, 4, 2, 4...]
    psum x1 -> x0, waiting for transfers between devices: 40.5 us -> none  [from_root(): return lax.psum(jnp.where(mine, shard, jnp.zeros_like(shard)), axis)]
    all_to_all x0 -> x1, blocking collectives: none -> 21.6 us  [on_device(): lax.all_to_all(outgoing, 'group', split_axis=0, concat_axis=0, tiled=True)]
    all_to_all x1 -> x0, waiting for transfers between devices: 8.57 us -> none  [on_device(): lax.all_to_all(outgoing, 'group', split_axis=0, concat_axis=0, tiled=True)]
    another operation x0 -> x3, local copies, waits for them, and re-layouts: none -> 7.6 us  [the longest x1 3.74 us: on_device(): pages[0].reshape(PREFIX_TOKENS, KEY_VALUE_HEADS, HEAD_DIMENSION)]
    dot_general x2, matrix products: 24.2 us -> 16.7 us  [the longest x1 10.3 us: on_device(): jnp.einsum('mk,skn->smn', both, win, preferred_element_type=jnp.float32)]
  transfers between devices with their start and end apart: 5 -> 2, of which waited for: 5 -> 1; matrix products, arithmetic and copies ran while one was open for 13% -> 2% of each run, Pallas kernels for 0% -> 0%
where the time goes in v1:
time: 221 us; the launch traced here: 220 us
  Pallas kernels  112 us (51%)
  matrix products  42.2 us (19%)
  blocking collectives  21.6 us (10%)
  local copies, waits for them, and re-layouts  21.1 us (10%)
  other arithmetic  19.5 us (9%)
    pallas_call x1, Pallas kernels, gather(): pl.pallas_call(gather_kernel, out_shape=(jax.ShapeDtypeStruct((2, 4, 2, 4...  112 us
    all_to_all x1, blocking collectives, on_device(): lax.all_to_all(outgoing, 'group', split_axis=0, concat_axis=0, tiled=True)  21.6 us
    dot_general x1, matrix products, on_device(): jnp.einsum('mk,skn->smn', both, win, preferred_element_type=jnp.float32)  10.3 us
    dot_general x2, matrix products, attend_update(): jnp.einsum('rkgn,nkd->rkgd', weights.astype(jnp.bfloat16), value_head_row...  10.1 us
    reduce_sum x2, other arithmetic, attend_update(): row_total = jnp.sum(weights, axis=-1)  9.58 us
    dot_general x1, matrix products, on_device(): jnp.einsum('rkgd,nkd->rkgn', query_groups, key_head_rows, preferred_eleme...  7 us
    dot_general x1, matrix products, on_device(): jnp.einsum('smn,snd->md', activated, wdown.reshape(32, 64, WIDTH), prefer...  6.45 us
    dot_general x1, matrix products, on_device(): jnp.dot(normed, query_key_value_weight, preferred_element_type=jnp.float32)  5.48 us
  transfers between devices with their start and end apart: 2, of which 1 were waited for; matrix products, arithmetic and copies ran while one was open for 2% of the time, Pallas kernels for 0%

profile of v1, /device:TPU:1, one launch (start us, length us, event | category | flops | bytes accessed | tf_op | source)
XLA Modules:
  0.0 220.3 jit_solution(14165547734674607785)
XLA Ops:
  1.5 1.5 fusion.45
  3.0 1.4 fusion.23
  5.2 5.5 %fusion.37 = f32[256,3072]{1,0:T(8,128)S(1)} fusion(bf16[1536,3072]{1,0:T(8,128)(2,1)} %param.13, bf16[256,1536]{1,0:T(8,128)(2,1)} %param.10, f32[1536]{0:T(1024)S(1)} %get-tuple-element.13, f32[256]{0:T(256)S(1)} %add_rsqrt_fusion.1), kind=kOutput, calls=%fused_computation.47 | convolution fusion | flops 2417491968 | bytes 13376512 | tf_op jit(solution)/shard_map/dot_general | solution.py:320
  10.8 1.0 slice.81
  12.6 1.2 compare_convert_fusion
  14.4 0.9 copy.33
  15.8 1.4 copy.32
  19.9 2.3 %fusion.13 = f32[8,96,256,2]{2,1,3,0:T(8,128)} fusion(bf16[256,8,96,1]{0,2,3,1:T(8,128)(2,1)S(1)} %bitcast.102, f32[8,256,256,2]{2,1,3,0:T(8,128)S(1)} %get-tuple-element.32, f32[256,8,2]{0,2,1:T(2,128)S(1)} %broadcast_maximum_fusion, pred[256,256]{0,1:T(8,128)(4,1)S(1)} %copy-done.13), kind=kOutput, calls=%fused_computation.23 | convolution fusion | flops 205520896 | bytes 6242304 | tf_op jit(solution)/shard_map/rkgn,nkd->rkgd/dot_general | solution.py:268
  23.8 1.0 pad_maximum_fusion.3.win
  25.5 111.9 %shard_map.116 = (bf16[2,4,2,4,32,768]{5,4,3,2,1,0:T(8,128)(2,1)}, bf16[4,2,4,1536,128]{4,3,2,1,0:T(8,128)(2,1)}, bf16[4,2,4,64,1536]{4,3,2,1,0:T(8,128)(2,1)}) custom-call(f32[4,1,768]{2,1,0:T(1,128)} %broadcast_in_dim.28.owned, bf16[2,32,768]{2,1,0:T(8,128)(2,1)} %pad_maximum_fusion.4.block, bf16[1536,128]{1,0:T(8,128)(2,1)} %pad_maximum_fusion.3.win, ...), custom_call_target="tpu_custom_call" | custom-call | tf_op jit(solution)/shard_map/pallas_call | solution.py:207
  137.4 3.3 %fusion.63 = (bf16[1,4,2,4,32,768]{5,4,3,2,1,0:T(8,128)(2,1)S(1)}, bf16[1,4,2,4,32,768]{5,4,3,2,1,0:T(8,128)(2,1)}) fusion(bf16[2,4,2,4,32,768]{5,4,3,2,1,0:T(8,128)(2,1)} %get-tuple-element.5), kind=kLoop, calls=%fused_computation.104 | loop fusion | bytes 6291456 | tf_op jit(solution)/shard_map/slice | solution.py:359
  140.7 3.2 %reshape_squeeze.6 = bf16[1024,8,96]{2,1,0:T(8,128)(2,1)} reshape(bf16[1,4,2,4,32,768]{5,4,3,2,1,0:T(8,128)(2,1)S(1)} %get-tuple-element.17) | data formatting | bytes 3145728 | tf_op jit(solution)/shard_map/reshape;squeeze | solution.py:359
  143.9 3.7 %reshape_squeeze.7 = bf16[1024,8,96]{2,1,0:T(8,128)(2,1)S(1)} reshape(bf16[1,4,2,4,32,768]{5,4,3,2,1,0:T(8,128)(2,1)} %get-tuple-element.18) | data formatting | bytes 3145728 | tf_op jit(solution)/shard_map/reshape;squeeze | solution.py:358
  147.7 7.0 %bitcast_reduce_fusion = (f32[256,8,2]{0,2,1:T(2,128)S(1)}, f32[8,1024,256,2]{2,1,3,0:T(8,128)}) fusion(bf16[256,8,2,48]{0,3,2,1:T(8,128)(2,1)S(1)} %bitcast.106, bf16[256,8,2,48]{0,3,2,1:T(8,128)(2,1)S(1)} %bitcast.104, bf16[1024,8,96,1]{2,1,0,3:T(8,128)(2,1)S(1)} %bitcast.95), kind=kOutput, calls=%fused_computation.1 | convolution fusion | flops 815263744 | bytes 19152896 | tf_op jit(solution)/shard_map/rkgd,nkd->rkgn/dot_general | solution.py:361
  154.7 8.7 %fusion.1 = f32[256,8,2]{0,2,1:T(2,128)S(1)} fusion(f32[8,1024,256,2]{2,1,3,0:T(8,128)} %get-tuple-element.34, f32[256,8,2]{0,2,1:T(2,128)S(1)} %broadcast_maximum_fusion.1), kind=kLoop, calls=%fused_computation.3 | loop fusion | flops 12578816 | bytes 16809984 | tf_op jit(solution)/shard_map/reduce_sum | solution.py:267
  163.5 7.9 %fusion.32 = bf16[256,8,2,96]{0,3,2,1:T(8,128)(2,1)S(1)} fusion(f32[8,96,256,2]{2,1,3,0:T(8,128)S(1)} %copy-done.7, f32[8,1024,256,2]{2,1,3,0:T(8,128)} %get-tuple-element.34, f32[256,8,2]{0,2,1:T(2,128)S(1)} %broadcast_maximum_fusion.1, bf16[1024,8,96,1]{2,1,0,3:T(8,128)(2,1)S(1)} %bitcast.101, f32[256,8,2]{0,2,1:T(2,128)S(1)} %get-tuple-element.14, ...), kind=kOutput, calls=%fused_computation.43 | convolution fusion | flops 819855360 | bytes 20774912 | tf_op jit(solution)/shard_map/rkgn,nkd->rkgd/dot_general | solution.py:268
  171.4 1.5 multiply_reduce_fusion
  172.9 1.1 multiply_convert_fusion
  174.0 1.7 collective-permute-start
  177.9 10.3 %convolution_bitcast_fusion.1 = f32[32,512,128]{1,2,0:T(8,128)S(1)} fusion(bf16[32,1536,128]{2,1,0:T(8,128)(2,1)} %bitcast.112, bf16[256,1536]{1,0:T(8,128)(2,1)} %collective-permute-done, bf16[256,1536]{1,0:T(8,128)(2,1)} %multiply_convert_fusion), kind=kOutput, calls=%fused_computation.15 | convolution fusion | flops 6445596672 | bytes 22544384 | tf_op jit(solution)/shard_map/mk,skn->smn/dot_general | solution.py:379
  188.2 6.4 %convolution_bitcast_fusion = f32[512,1536]{1,0:T(8,128)S(1)} fusion(bf16[32,64,1536]{2,1,0:T(8,128)(2,1)} %bitcast.113, f32[32,512,128]{1,2,0:T(8,128)S(1)} %convolution_bitcast_fusion.1), kind=kOutput, calls=%fused_computation.14 | convolution fusion | flops 3227516928 | bytes 17825792 | tf_op jit(solution)/shard_map/smn,snd->md/dot_general | solution.py:381
  195.8 21.6 %all_to_all.5 = bf16[4,8,16,1536]{3,1,2,0:T(8,128)(2,1)S(1)} all-to-all(bf16[4,8,16,1536]{3,1,2,0:T(8,128)(2,1)S(1)} %convolution_convert_fusion), channel_id=1, replica_groups=mesh['group'=4,'tensor'=32] {'group'}, dimensions={0} | all-to-all | bytes 3145728 | tf_op jit(solution)/shard_map/all_to_all | solution.py:408
  217.4 1.6 copy.40
  219.0 1.3 fusion.27
  (83 shorter events, 12.0 us)
Async XLA Ops:
  0.6 22.2 %copy-start = (bf16[128,1536]{1,0:T(8,128)(2,1)S(1)}, bf16[128,1536]{1,0:T(8,128)(2,1)}, u32[]{:S(2)}) copy-start(bf16[128,1536]{1,0:T(8,128)(2,1)} %param.16) | copy-start | bytes 1179652
  10.7 1.2 copy-start.19
  10.7 3.0 %copy-start.16 = (bf16[1,32,1536]{2,1,0:T(8,128)(2,1)S(1)}, bf16[1,32,1536]{2,1,0:T(8,128)(2,1)}, u32[]{:S(2)}) copy-start(bf16[1,32,1536]{2,1,0:T(8,128)(2,1)} %param.17) | copy-start | bytes 294916
  10.8 3.6 %copy-start.2 = (bf16[256,768]{1,0:T(8,128)(2,1)}, bf16[256,768]{1,0:T(8,128)(2,1)S(1)}, u32[]{:S(2)}) copy-start(bf16[256,768]{1,0:T(8,128)(2,1)S(1)} %slice.113) | copy-start | bytes 1179652
  17.2 0.8 copy-start.13
  17.7 1.2 copy-start.8
  17.7 1.2 copy-start.10
  18.9 1.0 copy-start.6
  19.9 2.3 %copy-start.14 = (bf16[1,32,768]{2,1,0:T(8,128)(2,1)S(1)}, bf16[1,32,768]{2,1,0:T(8,128)(2,1)}, u32[]{:S(2)}) copy-start(bf16[1,32,768]{2,1,0:T(8,128)(2,1)} %get-tuple-element.25) | copy-start | bytes 147460
  19.9 2.3 %copy-start.15 = (bf16[1,32,768]{2,1,0:T(8,128)(2,1)S(1)}, bf16[1,32,768]{2,1,0:T(8,128)(2,1)}, u32[]{:S(2)}) copy-start(bf16[1,32,768]{2,1,0:T(8,128)(2,1)} %get-tuple-element.26) | copy-start | bytes 147460
  19.9 3.6 %copy-start.12 = (bf16[2,1536,128]{2,1,0:T(8,128)(2,1)S(1)}, bf16[2,1536,128]{2,1,0:T(8,128)(2,1)}, u32[]{:S(2)}) copy-start(bf16[2,1536,128]{2,1,0:T(8,128)(2,1)} %param.15) | copy-start | bytes 2359300
  22.2 2.6 %copy-start.18 = (f32[4]{0:T(128)S(1)}, f32[4]{0:T(128)}, u32[]{:S(2)}) copy-start(f32[4]{0:T(128)} %compare_convert_fusion) | copy-start | bytes 52
  140.7 7.0 %copy-start.9 = (bf16[256,16,48]{0,2,1:T(8,128)(2,1)S(1)}, bf16[256,16,48]{0,2,1:T(8,128)(2,1)}, u32[]{:S(2)}) copy-start(bf16[256,16,48]{0,2,1:T(8,128)(2,1)} %copy-done.8) | copy-start | bytes 1179652
  140.7 7.0 %copy-start.11 = (bf16[256,16,48]{0,2,1:T(8,128)(2,1)S(1)}, bf16[256,16,48]{0,2,1:T(8,128)(2,1)}, u32[]{:S(2)}) copy-start(bf16[256,16,48]{0,2,1:T(8,128)(2,1)} %copy-done.10) | copy-start | bytes 1179652
  154.7 8.7 %copy-start.5 = (bf16[1024,8,96]{2,1,0:T(8,128)(2,1)S(1)}, bf16[1024,8,96]{2,1,0:T(8,128)(2,1)}, u32[]{:S(2)}) copy-start(bf16[1024,8,96]{2,1,0:T(8,128)(2,1)} %reshape_squeeze.6) | copy-start | bytes 4718596
  154.7 8.7 %copy-start.7 = (f32[8,96,256,2]{2,1,3,0:T(8,128)S(1)}, f32[8,96,256,2]{2,1,3,0:T(8,128)}, u32[]{:S(2)}) copy-start(f32[8,96,256,2]{2,1,3,0:T(8,128)} %fusion.13) | copy-start | bytes 4718596
  154.7 16.6 %slice-start = ((s8[4718592]{0:T(1024)(128)(4,1)}), s8[524288]{0:T(1024)(128)(4,1)S(1)}, s32[]{:S(2)}) async-start(s8[4718592]{0:T(1024)(128)(4,1)} %bitcast.93), calls=%async_computation.1 | async-start | bytes 1048576
  163.5 7.9 %slice-start.1 = ((s8[4718592]{0:T(1024)(128)(4,1)}), s8[4194304]{0:T(1024)(128)(4,1)S(1)}, s32[]{:S(2)}) async-start(s8[4718592]{0:T(1024)(128)(4,1)} %bitcast.93), calls=%async_computation.2 | async-start | bytes 8388608
  163.5 7.9 %copy-start.4 = (bf16[256,1536]{1,0:T(8,128)(2,1)S(1)}, bf16[256,1536]{1,0:T(8,128)(2,1)}, u32[]{:S(2)}) copy-start(bf16[256,1536]{1,0:T(8,128)(2,1)} %param.10) | copy-start | bytes 2359300
  171.4 4.3 %copy-start.17 = (s32[16,1]{0,1:T(1,128)S(1)}, s32[16,1]{0,1:T(1,128)}, u32[]{:S(2)}) copy-start(s32[16,1]{0,1:T(1,128)} %param.19) | copy-start | bytes 196
  171.4 4.5 %copy-start.3 = (bf16[256,768]{1,0:T(8,128)(2,1)S(1)}, bf16[256,768]{1,0:T(8,128)(2,1)}, u32[]{:S(2)}) copy-start(bf16[256,768]{1,0:T(8,128)(2,1)} %copy-done.2) | copy-start | bytes 1179652
  174.0 3.9 %collective-permute-start = (bf16[256,1536]{1,0:T(8,128)(2,1)}, bf16[256,1536]{1,0:T(8,128)(2,1)}, u32[]{:S(2)}, u32[]{:S(2)}) collective-permute-start(bf16[256,1536]{1,0:T(8,128)(2,1)} %multiply_convert_fusion), channel_id=1, source_target_pairs={{0,32},{32,0},{64,96},{96,64},{1,33},{33,1},{65,97},{97,65},{2,34}... | collective-permute-start | bytes 2359304 | tf_op jit(solution)/shard_map/ppermute | solution.py:288
  194.8 24.2 %collective-permute-start.1 = (f32[256,1536]{1,0:T(8,128)S(1)}, f32[256,1536]{1,0:T(8,128)S(1)}, u32[]{:S(2)}, u32[]{:S(2)}) collective-permute-start(f32[256,1536]{1,0:T(8,128)S(1)} %slice.88), channel_id=1, source_target_pairs={{0,32},{32,0},{64,96},{96,64},{1,33},{33,1},{65,97},{97,65},{2,34}... | collective-permute-start | bytes 4718600 | tf_op jit(solution)/shard_map/ppermute | solution.py:288
  217.4 2.9 %copy-start.1 = (bf16[128,1536]{1,0:T(8,128)(2,1)S(1)}, bf16[128,1536]{1,0:T(8,128)(2,1)}, u32[]{:S(2)}) copy-start(bf16[128,1536]{1,0:T(8,128)(2,1)} %param.16) | copy-start | bytes 1179652

commit v2 on v1

v2 whole, which is shorter than its diff:
```python
import functools

import jax
import jax.numpy as jnp
import numpy as np
from jax import lax
from jax.experimental import pallas as pl
from jax.experimental.pallas import tpu as pltpu
from jax.sharding import PartitionSpec as P

QUERY_HEADS = 16
KEY_VALUE_HEADS = 8
HEAD_DIMENSION = 96
PREFIX_TOKENS = 1024
CAP = 8
TOKENS = 256
PAGE = 16
WIDTH = 1536
HALF = 768
ROPE_BASE = 100000.0
EPSILON = 1e-05
NEGATIVE_FILLER = -1e30
MESH = pl.DeviceIdType.MESH
F32, BF16 = jnp.float32, jnp.bfloat16


N_Z, N_H, N_Y = 4, 2, 4
DIRECTIONS = ("x", "y+", "y-", "z+", "z-", "sib")
ALL = slice(None)


class Plan:
    def __init__(self):
        self.copies = []

    def add(self, buffer, source, target, direction, after, size):
        self.copies.append((buffer, source, target, direction, tuple(after), size))
        return len(self.copies) - 1

    def ring(self, buffer, axis, after, block, size):
        up = self.add(buffer, block(0, None), block(3, None), axis + "+", after, size)
        down = self.add(buffer, block(0, None), block(1, None), axis + "-", after, size)
        far_up = self.add(buffer, block(3, 0), block(2, 0), axis + "+", [up], size / 2)
        far_down = self.add(buffer, block(1, 1), block(2, 1), axis + "-", [down], size / 2)
        return [up, down, far_up, far_down]

    def piece(self, buffer, order, cut, size, after=()):
        index = lambda z, h, y, part: (z, h, y) + cut(part)
        done = []
        if order[0] == "x":
            swap = self.add(buffer, index(0, 0, 0, None), index(0, 1, 0, None), "x", after, size)
            done.append(swap)
            for h, first in ((0, list(after)), (1, [swap])):
                if order[1] == "y":
                    near = self.ring(buffer, "y", first, lambda d, p, h=h: index(0, h, d, p), size)
                    far = self.ring(buffer, "z", near, lambda d, p, h=h: index(d, h, ALL, p), 4 * size)
                else:
                    near = self.ring(buffer, "z", first, lambda d, p, h=h: index(d, h, 0, p), size)
                    far = self.ring(buffer, "y", near, lambda d, p, h=h: index(ALL, h, d, p), 4 * size)
                done += near + far
        else:
            if order[0] == "y":
                near = self.ring(buffer, "y", list(after), lambda d, p: index(0, 0, d, p), size)
                far = self.ring(buffer, "z", near, lambda d, p: index(d, 0, ALL, p), 4 * size)
                at = lambda d, h: index(d, h, ALL, None)
            else:
                near = self.ring(buffer, "z", list(after), lambda d, p: index(d, 0, 0, p), size)
                far = self.ring(buffer, "y", near, lambda d, p: index(ALL, 0, d, p), 4 * size)
                at = lambda d, h: index(ALL, h, d, None)
            done += near + far
            for d, need in ((0, near), (3, far[:1]), (1, far[1:2]), (2, far[2:])):
                done.append(self.add(buffer, at(d, 0), at(d, 1), "x", need, 4 * size))
        return done

    def order(self, work=(), link=46.0, chip=250.0, latency=1600.0):
        free = {d: 0.0 for d in DIRECTIONS}
        arrival, issued, now = {}, [], 0.0
        left, work = list(range(len(self.copies))), list(work)

        def known(needs):
            return all(d in arrival for d in needs)

        while left or work:
            ready = {k: max([0.0] + [arrival[d] for d in self.copies[k][4]]) for k in left if known(self.copies[k][4])}
            pick = min(ready, key=lambda k: (max(ready[k], now), k)) if ready else None
            if pick is not None and ready[pick] <= now:
                direction, size = self.copies[pick][3], self.copies[pick][5]
                free[direction] = max(now, free[direction]) + size / (chip if direction == "sib" else link)
                arrival[pick] = free[direction] + latency
                issued.append(("copy", pick))
                left.remove(pick)
                continue
            start = max([0.0] + [arrival[d] for d in work[0][2]]) if work and known(work[0][2]) else None
            if start is not None and (pick is None or start <= max(now, ready[pick])):
                now = max(now, start) + work[0][1]
                issued.append(("work", work.pop(0)))
                continue
            now = ready[pick]
        return issued, arrival, now


def gather_plan():
    plan = Plan()

    def prefix_cut(first):
        return lambda part: (
            pl.ds(first, 16),
            pl.ds(0, HALF) if part is None else pl.ds(384 * part, 384),
        )

    def row_cut(first, count):
        return lambda part: (
            pl.ds(first, count) if part is None else pl.ds(first + count // 2 * part, count // 2),
            ALL,
        )

    done = plan.piece("prefix", "xyz", prefix_cut(0), 16 * HALF * 2)
    done += plan.piece("prefix", "xzy", prefix_cut(16), 16 * HALF * 2)
    share = plan.add("prefix", (), (), "sib", done, 32 * 32 * HALF * 2)
    plan.piece("in", "xyz", row_cut(0, HALF), HALF * 256)
    plan.piece("in", "xzy", row_cut(HALF, HALF), HALF * 256)
    plan.piece("down", "yzx", row_cut(0, 32), 32 * WIDTH * 2)
    plan.piece("down", "zyx", row_cut(32, 32), 32 * WIDTH * 2)
    return plan, [share] + done


def covers(plan, z, high):
    fits = lambda index, at: index == ALL or index == at
    return [
        k
        for k, (name, _, target, _, _, _) in enumerate(plan.copies)
        if name != "prefix" and fits(target[0], z) and fits(target[1], high)
    ]


def neighbours():
    g, t = lax.axis_index("group"), lax.axis_index("tensor")
    core, low = g % 2, g // 2
    y, high, z = t % 4, (t // 4) % 2, t // 8

    def at(zz, hh, yy):
        return (zz % 4) * 8 + hh * 4 + yy % 4

    return {
        "x": ((1 - low) * 2 + core, at(z, 1 - high, y)),
        "y+": (g, at(z, high, y + 1)),
        "y-": (g, at(z, high, y + 3)),
        "z+": (g, at(z + 1, high, y)),
        "z-": (g, at(z + 3, high, y)),
        "sib": (low * 2 + 1 - core, t),
        "twin": ((1 - low) * 2 + core, t),
        "cross": ((1 - low) * 2 + 1 - core, t),
    }


def rope_table():
    half = HEAD_DIMENSION // 2
    frequency = (ROPE_BASE ** (-np.arange(half, dtype=np.float32) / half)).astype(np.float32)
    angles = (PREFIX_TOKENS + np.arange(128, dtype=np.float32))[None, :] * frequency[:, None]
    rest = np.concatenate([np.cos(angles.astype(np.float64)), np.sin(angles.astype(np.float64))]).astype(np.float32)
    parts = []
    for _ in range(3):
        parts.append(rest.astype(jnp.bfloat16))
        rest = rest - parts[-1].astype(np.float32)
    return np.concatenate(parts)


def norm_rows(values, gain):
    return values * lax.rsqrt(jnp.mean(values * values, axis=-1, keepdims=True) + EPSILON) * gain


def dot(left, right):
    return jnp.dot(left, right, preferred_element_type=F32)


def layer_kernel(
    hidden, segment_ref, gains, owner_ref, dest_ref, table, qkv_hbm, out_hbm, in_hbm, down_hbm, prefix_hbm,
    result, suffix,
    raw, block, rival, win, wdown, pages, qkv, w_out, cache, heads, mixed, turn, mask, outgoing, tokens, middle,
    normed, total, sent, received,
    local, cand_send, cand_recv, send, recv, swap_send, swap_recv, page_send, page_recv,
):
    group = lax.axis_index("group")
    core = group % 2
    near = neighbours()
    plan, prefix_done = gather_plan()

    def fetch(source, target, slot):
        copy = pltpu.make_async_copy(source, target, local.at[slot])
        copy.start()
        return copy

    columns = lambda at: pl.ds(pl.multiple_of(at * HALF, 128), HALF)
    first = [fetch(prefix_hbm.at[0, :, pl.ds(HALF * n, HALF)], block.at[n], n) for n in range(2)]
    weights = [fetch(in_hbm, raw, 2)]
    own = [fetch(down_hbm.at[pl.ds(pl.multiple_of(64 * core, 64), 64), :], wdown.at[0, 0, 0], 3)]
    loads = [fetch(qkv_hbm.at[:, pl.ds(384 * n, 384)], qkv.at[n], 4 + n) for n in range(8)]
    out_load = fetch(out_hbm, w_out, 12)

    barrier = pltpu.get_barrier_semaphore()
    for target in near.values():
        pl.semaphore_signal(barrier, inc=1, device_id=target, device_id_type=MESH)
    for copy in first:
        copy.wait()
    pl.semaphore_wait(barrier, len(near))

    rivals = [
        pltpu.make_async_remote_copy(
            src_ref=block.at[half],
            dst_ref=rival.at[slot],
            send_sem=cand_send.at[slot],
            recv_sem=cand_recv.at[slot],
            device_id=near[name],
            device_id_type=MESH,
        )
        for slot, (name, half) in enumerate((("sib", 1 - core), ("twin", core), ("cross", 1 - core)))
    ]
    for copy in rivals:
        copy.start()

    weights[0].wait()
    gate, up = raw[0].astype(F32), raw[1].astype(F32)
    low_lane = lax.broadcasted_iota(jnp.int32, (WIDTH, 128), 1) < 64
    left = jnp.where(core == 0, gate, pltpu.roll(gate, 64, 1))
    right = jnp.where(core == 0, pltpu.roll(up, 64, 1), up)
    win[0, 0, 0] = jnp.where(low_lane, left, right).astype(BF16)

    tensor = lax.axis_index("tensor")
    owners = owner_ref[...]
    lanes = lax.broadcasted_iota(jnp.int32, owners.shape, 1)
    owner = jnp.sum(jnp.where(lanes == tensor, owners, 0), axis=1, keepdims=True)
    low = group // 2
    names = (group, low * 2 + 1 - core, (1 - low) * 2 + core, (1 - low) * 2 + 1 - core)
    chosen = jnp.where(owner == names[0], block[core], jnp.zeros((32, HALF), BF16))
    for slot, copy in enumerate(rivals):
        copy.wait_recv()
        chosen = jnp.where(owner == names[slot + 1], rival[slot], chosen)
    pages[core, 0, 0, 0] = chosen
    own[0].wait()

    def place(name, index):
        if name == "prefix":
            return pages.at[core].at[index] if index else pages.at[core]
        return {"in": win, "down": wdown}[name].at[index]

    def swap(source, target, slot, name, sems, arrivals):
        return pltpu.make_async_remote_copy(
            src_ref=source, dst_ref=target, send_sem=sems.at[slot], recv_sem=arrivals.at[slot],
            device_id=near[name], device_id_type=MESH,
        )

    swaps, page_copies, page_own = [], [], []

    def prepare():
        values = hidden[...].astype(F32)
        normed[...] = norm_rows(values, gains[0:1]).astype(BF16)
        segment = segment_ref[...].astype(F32)
        across = jnp.broadcast_to(segment, (TOKENS, TOKENS))
        key = lax.broadcasted_iota(jnp.int32, (TOKENS, TOKENS), 0)
        query = lax.broadcasted_iota(jnp.int32, (TOKENS, TOKENS), 1)
        allowed = jnp.where((across.T == across) & (key <= query), 1.0, 0.0)
        mask[...] = allowed
        offset = (jnp.sum(allowed, axis=0, keepdims=True) - 1.0).astype(jnp.int32)
        spot = lax.broadcasted_iota(jnp.int32, (128, TOKENS), 0) == offset
        parts = dot(table[...], jnp.where(spot, 1.0, 0.0).astype(BF16))
        turn[...] = parts[0:96] + parts[96:192] + parts[192:288]

    def rotate(rows):
        cosine, sine = turn[0:48], turn[48:96]
        out = []
        for n in range(4):
            one, two = rows[96 * n : 96 * n + 48], rows[96 * n + 48 : 96 * n + 96]
            out += [one * cosine - two * sine, two * cosine + one * sine]
        return out

    def project(n):
        loads[n].wait()
        projected = dot(normed[...], qkv[n])
        if n < 4:
            turned = rotate(projected.T)
            for m in range(4):
                heads[4 * n + m] = jnp.concatenate(turned[2 * m : 2 * m + 2], axis=0).astype(BF16)
        elif n < 6:
            cache[:, 384 * (n - 4) : 384 * (n - 3)] = jnp.concatenate(rotate(projected.T), axis=0).T.astype(BF16)
        else:
            cache[:, 384 * (n - 4) : 384 * (n - 3)] = projected.astype(BF16)

    def send_pages():
        page = lax.broadcasted_iota(jnp.int32, (PAGE, TOKENS), 0)
        token = lax.broadcasted_iota(jnp.int32, (PAGE, TOKENS), 1)
        dest = jnp.broadcast_to(dest_ref[...], (PAGE, TOKENS))
        along = jnp.sum(jnp.where(token // PAGE == page, dest, 0), axis=0, keepdims=True)
        earlier = jnp.where((dest == along) & (page < token // PAGE), 1, 0)
        rank = jnp.sum(earlier, axis=0, keepdims=True)
        row = along * (CAP * PAGE) + rank * PAGE + token[0:1] % PAGE
        pick = lax.broadcasted_iota(jnp.int32, (4 * CAP * PAGE, TOKENS), 0) == row
        outgoing[...] = dot(jnp.where(pick, 1.0, 0.0).astype(BF16), cache[...]).astype(BF16).reshape(4, CAP * PAGE, WIDTH)
        page_own.append(fetch(outgoing.at[group], suffix.at[group], 13))
        for slot, name in enumerate(("sib", "twin", "cross")):
            copy = swap(outgoing.at[near[name][0]], suffix.at[group], slot, name, page_send, page_recv)
            copy.start()
            page_copies.append(copy)

    def attend(n):
        start = 96 * n // 128 * 128
        skip = 96 * n - start
        wide = 128 if skip + 96 <= 128 else 256
        query = jnp.concatenate([heads[2 * n], heads[2 * n + 1]], axis=1)
        rows = [query]
        if skip:
            rows = [jnp.zeros((skip, 2 * TOKENS), BF16)] + rows
        if wide - skip - 96:
            rows = rows + [jnp.zeros((wide - skip - 96, 2 * TOKENS), BF16)]
        query = jnp.concatenate(rows, axis=0)
        window = slice(start, start + wide)
        scores = [dot(pages[0, z, :, :, :, window].reshape(256, wide), query) for z in range(4)]
        allowed = mask[...]
        allowed = jnp.concatenate([allowed, allowed], axis=1) > 0.5
        scores.append(jnp.where(allowed, dot(cache[:, window], query), NEGATIVE_FILLER))
        values = [pages[1, z, :, :, :, window].reshape(256, wide) for z in range(4)]
        values.append(cache[:, slice(HALF + start, HALF + start + wide)])
        top = scores[0].max(axis=0, keepdims=True)
        for part in scores[1:]:
            top = jnp.maximum(top, part.max(axis=0, keepdims=True))
        scale = HEAD_DIMENSION ** (-0.5) * 1.4426950408889634
        whole, summed = None, None
        for part, value in zip(scores, values):
            weight = jnp.exp2((part - top) * scale)
            mass = jnp.sum(weight, axis=0, keepdims=True)
            product = lax.dot_general(
                value, weight.astype(BF16), (((0,), (0,)), ((), ())), preferred_element_type=F32
            )
            whole = mass if whole is None else whole + mass
            summed = product if summed is None else summed + product
        out = summed[skip : skip + 96] / whole
        mixed[2 * n] = out[:, :TOKENS]
        mixed[2 * n + 1] = out[:, TOKENS:]

    def leave():
        out_load.wait()
        attended = mixed[...].reshape(WIDTH, TOKENS).T.astype(BF16)
        summed = (hidden[...].astype(F32) + dot(attended, w_out[...])).astype(BF16)
        middle[...] = summed
        tokens[0] = norm_rows(summed.astype(F32), gains[1:2]).astype(BF16)
        copy = swap(tokens.at[0], tokens.at[1], 0, "sib", swap_send, swap_recv)
        copy.start()
        swaps.append(copy)
        total[...] = jnp.zeros_like(total)

    def feed(z, high):
        if (z, high) == (0, 0):
            swaps[0].wait_recv()
        both = tokens[...].reshape(2 * TOKENS, WIDTH)
        low_half = lax.broadcasted_iota(jnp.int32, (2 * TOKENS, 128), 1) < 64
        active = []
        for pair in range(2):
            joined = jnp.concatenate([win[z, high, 2 * pair], win[z, high, 2 * pair + 1]], axis=1)
            product = dot(both, joined)
            one, two = product[:, :128], product[:, 128:]
            gate_part = jnp.where(low_half, one, pltpu.roll(two, 64, 1))
            up_part = jnp.where(low_half, pltpu.roll(one, 64, 1), two)
            active.append((gate_part / (1.0 + jnp.exp(-gate_part)) * up_part).astype(BF16))
        total[...] += dot(jnp.concatenate(active, axis=1), wdown[z, high].reshape(256, WIDTH))

    def finish():
        sent[...] = total[TOKENS:].astype(BF16)
        copy = swap(sent, received, 1, "sib", swap_send, swap_recv)
        copy.start()
        swaps.append(copy)
        mine = middle[...].astype(F32) + total[:TOKENS]
        copy.wait_recv()
        result[...] = (mine + received[...].astype(F32)).astype(BF16)

    work = [(prepare, 2000.0, ())]
    work += [(functools.partial(project, n), 1000.0, ()) for n in range(8)]
    work += [(send_pages, 2000.0, ())]
    work += [(functools.partial(attend, n), 2500.0, prefix_done) for n in range(8)]
    work += [(leave, 4000.0, ())]
    work += [(functools.partial(feed, z, high), 2500.0, covers(plan, z, high)) for high in range(2) for z in range(4)]
    work += [(finish, 3000.0, ())]

    copies, arrived = {}, set()

    def await_all(needs):
        for k in needs:
            if k not in arrived:
                copies[k].wait_recv()
                arrived.add(k)

    order, _, _ = plan.order(work)
    for kind, item in order:
        if kind == "work":
            await_all(item[2])
            item[0]()
            continue
        name, source, target, direction, after, _ = plan.copies[item]
        await_all(after)
        copies[item] = swap(place(name, source), place(name, target), item, direction, send, recv)
        copies[item].start()
    await_all(range(len(plan.copies)))
    for copy in copies.values():
        copy.wait_send()
    for copy in rivals + swaps:
        copy.wait_send()
    for copy in page_copies:
        copy.wait()
    page_own[0].wait()


def layer(*operands):
    count = len(gather_plan()[0].copies)
    vmem = pl.BlockSpec(memory_space=pltpu.VMEM)
    anywhere = pl.BlockSpec(memory_space=pl.ANY)
    dma = pltpu.SemaphoreType.DMA
    return pl.pallas_call(
        layer_kernel,
        out_shape=(
            jax.ShapeDtypeStruct((TOKENS, WIDTH), BF16),
            jax.ShapeDtypeStruct((4, CAP * PAGE, WIDTH), BF16),
        ),
        in_specs=[vmem] * 6 + [anywhere] * 5,
        out_specs=(vmem, anywhere),
        scratch_shapes=[
            pltpu.VMEM((2, WIDTH, 128), BF16),
            pltpu.VMEM((2, 32, HALF), BF16),
            pltpu.VMEM((3, 32, HALF), BF16),
            pltpu.VMEM((4, 2, 4, WIDTH, 128), BF16),
            pltpu.VMEM((4, 2, 4, 64, WIDTH), BF16),
            pltpu.VMEM((2, 4, 2, 4, 32, HALF), BF16),
            pltpu.VMEM((8, WIDTH, 384), BF16),
            pltpu.VMEM((WIDTH, WIDTH), BF16),
            pltpu.VMEM((TOKENS, WIDTH), BF16),
            pltpu.VMEM((QUERY_HEADS, HEAD_DIMENSION, TOKENS), BF16),
            pltpu.VMEM((QUERY_HEADS, HEAD_DIMENSION, TOKENS), F32),
            pltpu.VMEM((HEAD_DIMENSION, TOKENS), F32),
            pltpu.VMEM((TOKENS, TOKENS), F32),
            pltpu.VMEM((4, CAP * PAGE, WIDTH), BF16),
            pltpu.VMEM((2, TOKENS, WIDTH), BF16),
            pltpu.VMEM((TOKENS, WIDTH), BF16),
            pltpu.VMEM((TOKENS, WIDTH), BF16),
            pltpu.VMEM((2 * TOKENS, WIDTH), F32),
            pltpu.VMEM((TOKENS, WIDTH), BF16),
            pltpu.VMEM((TOKENS, WIDTH), BF16),
            dma((14,)), dma((3,)), dma((3,)), dma((count,)), dma((count,)), dma((2,)), dma((2,)), dma((3,)), dma((3,)),
        ],
        compiler_params=pltpu.CompilerParams(
            collective_id=0, has_side_effects=True, vmem_limit_bytes=67043328
        ),
    )(*operands)


def on_device(
    hidden_in,
    request_ids,
    norm_gains,
    query_key_value_weight,
    w_out,
    w_in,
    w_down,
    prefix_cache,
    prefix_owner,
    page_dest,
):
    hidden_out, suffix = layer(
        hidden_in, request_ids, norm_gains, prefix_owner.reshape(1, -1), page_dest, jnp.asarray(rope_table()),
        query_key_value_weight, w_out, w_in, w_down, prefix_cache,
    )
    return (hidden_out, suffix.reshape(1, 1, 4, CAP, PAGE, WIDTH))


def solution(mesh):
    return jax.shard_map(
        on_device,
        mesh=mesh,
        in_specs=(
            P(("group", "tensor"), None),
            P(("group", "tensor"), None),
            P(),
            P(),
            P(),
            P(None, None, "tensor"),
            P("tensor", None),
            P("group", "tensor", None),
            P(),
            P(("group", "tensor"), None),
        ),
        out_specs=(P(("group", "tensor"), None), P("group", "tensor", None, None, None, None)),
        check_vma=False,
    )
```

time: 221 us -> 129 us (0.58)
  matrix products: 42.2 us -> 0 us
  blocking collectives: 21.6 us -> 0 us
  other arithmetic: 19.5 us -> 0 us
  local copies, waits for them, and re-layouts: 21.1 us -> 6.04 us
  Pallas kernels: 112 us -> 122 us
    dot_general x9 -> x0, matrix products: 42.2 us -> none  [the longest x1 10.3 us: on_device(): jnp.einsum('mk,skn->smn', both, win, preferred_element_type=jnp.float32)]
    all_to_all x1 -> x0, blocking collectives: 21.6 us -> none  [on_device(): lax.all_to_all(outgoing, 'group', split_axis=0, concat_axis=0, tiled=True)]
    reduce_sum x4 -> x0, other arithmetic: 11.1 us -> none  [the longest x2 9.58 us: attend_update(): row_total = jnp.sum(weights, axis=-1)]
    pallas_call x1, Pallas kernels: 112 us -> 122 us  [layer(): pl.pallas_call(layer_kernel, out_shape=(jax.ShapeDtypeStruct((TOKENS, WID...]
    another operation x3 -> x0, local copies, waits for them, and re-layouts: 7.6 us -> none  [the longest x1 3.74 us: on_device(): pages[0].reshape(PREFIX_TOKENS, KEY_VALUE_HEADS, HEAD_DIMENSION)]
    slice x8 -> x0, local copies, waits for them, and re-layouts: 7.29 us -> none  [the longest x1 3.32 us: on_device(): pages[1].reshape(PREFIX_TOKENS, KEY_VALUE_HEADS, HEAD_DIMENSION)]
    unnamed x45 -> x3, local copies, waits for them, and re-layouts: 1.97 us -> 6.04 us
    convert_element_type x5 -> x0, other arithmetic: 3.59 us -> none  [the longest x1 1.27 us: on_device(): hidden_out = (middle.astype(jnp.float32) + mlp_out).astype(jnp.bfloat16)]
  transfers between devices with their start and end apart: 2 -> 0, of which waited for: 1 -> 0; matrix products, arithmetic and copies ran while one was open for 2% -> 0% of each run, Pallas kernels for 0% -> 0%
where the time goes in v2:
time: 129 us; the launch traced here: 128 us
  Pallas kernels  122 us (95%)
  local copies, waits for them, and re-layouts  6.04 us (5%)
    pallas_call x1, Pallas kernels, layer(): pl.pallas_call(layer_kernel, out_shape=(jax.ShapeDtypeStruct((TOKENS, WID...  122 us
    unnamed x3, local copies, waits for them, and re-layouts  6.04 us

profile of v2, /device:TPU:1, one launch (start us, length us, event | category | flops | bytes accessed | tf_op | source)
XLA Modules:
  0.0 128.4 jit_solution(10537337676849450024)
XLA Ops:
  0.6 1.3 %copy.13.dest_ref = s32[16,1]{1,0:T(8,128)} copy(s32[16,1]{0,1:T(1,128)} %param.20) | data formatting | bytes 128 | tf_op args[9]
  2.0 121.7 %shard_map.122 = (bf16[256,1536]{1,0:T(8,128)(2,1)}, bf16[4,128,1536]{2,1,0:T(8,128)(2,1)}) custom-call(bf16[256,1536]{1,0:T(8,128)(2,1)} %hidden.1, s32[1,256]{1,0:T(1,128)} %segment_ref.1, f32[2,1536]{1,0:T(2,128)} %gains.1, s32[1,32]{1,0:T(1,128)} %bitcast.3, s32[16,1]{1,0:T(8,128)} %copy.13.dest_ref, bf16[288,128]{1,0:T(8,128)(2,1)} %constant.2.clone.table, ...), custom_call_target="tpu_custom_call" | custom-call | tf_op jit(solution)/shard_map/pallas_call | solution.py:415
  123.7 2.1 %copy.16 = bf16[256,1536]{1,0:T(8,128)(2,1)} copy(bf16[256,1536]{1,0:T(8,128)(2,1)} %get-tuple-element.8) | data formatting | bytes 1572864
  125.8 2.7 %copy.17 = bf16[1,1,4,8,16,1536]{5,4,3,2,1,0:T(8,128)(2,1)} copy(bf16[1,1,4,8,16,1536]{5,4,3,2,1,0:T(8,128)(2,1)} %bitcast.2) | data formatting | bytes 3145728
